TPU v7x, 32 devices: a whole 2x2x4 slice. The times are simulated.
32 devices in a mesh: row: 16 (over z, x, core), col: 2 (over y).
Axes of the slice: x: 2, y: 2, z: 4, core: 2. Of those that a mesh axis runs over, the one named last changes fastest.
Arguments:
- qkv: bfloat16 [256, 16, 3, 3072], P('row', 'col'), may hold values from -6 to 6
- cotangent: bfloat16 [256, 16, 3072], P('row', 'col'), may hold values from -6 to 6
- norm_gains: float32 [2, 128], replicated, may hold values from 0.1 to 1.9
- rel_table: float32 [24, 15, 15], replicated, may hold values from -6 to 250
- shifts: int32 [2], replicated, may hold values from 1 to 7
- mask_ids: int32 [256, 16], replicated, may hold values from 0 to 2
Outputs:
- attention: bfloat16 [256, 16, 3072], P('row', 'col')
- d_qkv: bfloat16 [256, 16, 3, 3072], P('row', 'col')
- d_gains: float32 [2, 128], replicated
- d_table: float32 [24, 15, 15], replicated
All inputs are finite; a program needn't handle non-finite values.
Results may differ from a plain program's by a relative error of at most 0.0073.
Values may be sent and summed in bfloat16 or wider, within the bound.
A program may use at most 192 MiB of HBM per device.

v0:
```python
import math
import jax
import jax.numpy as jnp
from jax import lax
from jax.sharding import PartitionSpec as P

EPSILON = 1e-06
NEG_FILL = -1e30


def shifted(value, axis, steps):
    count = lax.axis_size(axis)
    pairs = [(source, (source + steps) % count) for source in range(count)]
    return lax.ppermute(value, axis, pairs)


def head_norm(inputs, gain_vec):
    values = inputs.astype(jnp.float32)
    average = jnp.mean(values, axis=-1, keepdims=True)
    centred = values - average
    variance = jnp.mean(centred * centred, axis=-1, keepdims=True)
    inv_sigma = lax.rsqrt(variance + EPSILON)
    x_hat = centred * inv_sigma
    return (x_hat, inv_sigma, (x_hat * gain_vec).astype(jnp.bfloat16))


def norm_back(x_hat, inv_sigma, d_normed, gain_vec):
    d_hat = d_normed * gain_vec
    first_mean = jnp.mean(d_hat, axis=-1, keepdims=True)
    second_mean = jnp.mean(d_hat * x_hat, axis=-1, keepdims=True)
    d_input = inv_sigma * (d_hat - first_mean - x_hat * second_mean)
    d_gain = jnp.sum(d_normed * x_hat, axis=tuple(range(d_normed.ndim - 1)))
    return (d_input, d_gain)


def offset_table(window_size):
    span_count = 2 * window_size - 1
    places = jnp.arange(window_size * window_size, dtype=jnp.int32)
    row_pos = places // window_size
    col_pos = places % window_size
    code_grid = (row_pos[:, None] - row_pos[None, :] + window_size - 1) * span_count + (
        col_pos[:, None] - col_pos[None, :] + window_size - 1
    )
    codes = jnp.arange(span_count * span_count, dtype=jnp.int32)
    return (code_grid[:, :, None] == codes[None, None, :]).astype(jnp.float32)


def to_windows(field, window_size):
    row_count, col_count = (field.shape[0], field.shape[1])
    trailing = field.shape[2:]
    blocks = field.reshape(
        (row_count // window_size, window_size, col_count // window_size, window_size) + trailing
    )
    blocks = jnp.moveaxis(blocks, 2, 1)
    return blocks.reshape(
        (row_count // window_size * (col_count // window_size), window_size * window_size)
        + trailing
    )


def from_windows(blocks, window_size, row_count, col_count):
    trailing = blocks.shape[2:]
    field = blocks.reshape(
        (row_count // window_size, col_count // window_size, window_size, window_size) + trailing
    )
    field = jnp.moveaxis(field, 1, 2)
    return field.reshape((row_count, col_count) + trailing)


def window_core(q_norm, k_norm, values, grads, pos_bias, allowed, score_scale):
    scores = (
        jnp.einsum("wqhd,wkhd->whqk", q_norm, k_norm, preferred_element_type=jnp.float32)
        * score_scale
        + pos_bias[None]
    )
    scores = jnp.where(allowed[:, None], scores, NEG_FILL)
    row_max = jnp.max(scores, axis=-1, keepdims=True)
    weights = jnp.exp(scores - row_max)
    probs = weights / jnp.sum(weights, axis=-1, keepdims=True)
    probs_b = probs.astype(jnp.bfloat16)
    output = jnp.einsum("whqk,wkhd->wqhd", probs_b, values, preferred_element_type=jnp.float32)
    d_probs = jnp.einsum("wqhd,wkhd->whqk", grads, values, preferred_element_type=jnp.float32)
    row_dot = jnp.sum(probs * d_probs, axis=-1, keepdims=True)
    d_scores = probs * (d_probs - row_dot)
    d_scores_b = d_scores.astype(jnp.bfloat16)
    d_qnorm = (
        jnp.einsum("whqk,wkhd->wqhd", d_scores_b, k_norm, preferred_element_type=jnp.float32)
        * score_scale
    )
    d_knorm = (
        jnp.einsum("whqk,wqhd->wkhd", d_scores_b, q_norm, preferred_element_type=jnp.float32)
        * score_scale
    )
    d_value = jnp.einsum("whqk,wqhd->wkhd", probs_b, grads, preferred_element_type=jnp.float32)
    return (output, d_qnorm, d_knorm, d_value, jnp.sum(d_scores, axis=0))


def label_pairs(labels, window_size):
    label_win = to_windows(labels, window_size)
    return label_win[:, :, None] == label_win[:, None, :]


def local(qkv, cotangent, norm_gains, rel_table, shifts, mask_ids):
    tile_rows, tile_cols = (qkv.shape[0], qkv.shape[1])
    feature_width = qkv.shape[3]
    head_count = rel_table.shape[0]
    head_dim = feature_width // head_count
    span_count = rel_table.shape[1]
    window_size = (span_count + 1) // 2
    score_scale = 1.0 / math.sqrt(head_dim)
    shift_row = shifts[0]
    shift_col = shifts[1]
    grid_row = lax.axis_index("row") * tile_rows
    grid_col = lax.axis_index("col") * tile_cols
    one_hot = offset_table(window_size)
    pos_bias = jnp.einsum(
        "hc,qkc->hqk",
        rel_table.reshape(head_count, span_count * span_count),
        one_hot,
        precision=lax.Precision.HIGHEST,
    )
    gain_q = norm_gains[0]
    gain_k = norm_gains[1]
    stacked = jnp.concatenate([qkv, cotangent[:, :, None]], axis=2)
    received = shifted(stacked[:window_size], "row", -1)
    rolled = lax.dynamic_slice_in_dim(
        jnp.concatenate([stacked, received], axis=0), shift_row, tile_rows, 0
    )
    received = shifted(rolled, "col", -1)
    rolled = lax.dynamic_slice_in_dim(
        jnp.concatenate([rolled, received], axis=1), shift_col, tile_cols, 1
    )
    fields = rolled.reshape(tile_rows, tile_cols, 4, head_count, head_dim)
    q_hat, q_inv, q_norm = head_norm(fields[:, :, 0], gain_q)
    k_hat, k_inv, k_norm = head_norm(fields[:, :, 1], gain_k)
    labels = jnp.roll(mask_ids, (-(grid_row + shift_row), -(grid_col + shift_col)), (0, 1))[
        :tile_rows, :tile_cols
    ]
    output, d_qnorm, d_knorm, d_value, d_bias = window_core(
        to_windows(q_norm, window_size),
        to_windows(k_norm, window_size),
        to_windows(fields[:, :, 2], window_size),
        to_windows(fields[:, :, 3], window_size),
        pos_bias,
        label_pairs(labels, window_size),
        score_scale,
    )
    output = from_windows(output, window_size, tile_rows, tile_cols)
    d_qnorm = from_windows(d_qnorm, window_size, tile_rows, tile_cols)
    d_knorm = from_windows(d_knorm, window_size, tile_rows, tile_cols)
    d_value = from_windows(d_value, window_size, tile_rows, tile_cols)
    d_query, dgain_q = norm_back(q_hat, q_inv, d_qnorm, gain_q)
    d_key, dgain_k = norm_back(k_hat, k_inv, d_knorm, gain_k)
    results = (
        jnp.stack([output, d_query, d_key, d_value], axis=2)
        .reshape(tile_rows, tile_cols, 4, feature_width)
        .astype(jnp.bfloat16)
    )
    received = shifted(results[tile_rows - window_size :], "row", 1)
    results = lax.dynamic_slice_in_dim(
        jnp.concatenate([received, results], axis=0), window_size - shift_row, tile_rows, 0
    )
    received = shifted(results, "col", 1)
    results = lax.dynamic_slice_in_dim(
        jnp.concatenate([received, results], axis=1), window_size - shift_col, tile_cols, 1
    )
    attention = results[:, :, 0]
    d_qkv = results[:, :, 1:]
    table_local = jnp.einsum("hqk,qkc->hc", d_bias, one_hot, precision=lax.Precision.HIGHEST)
    totals = lax.psum((jnp.stack([dgain_q, dgain_k]), table_local), ("row", "col"))
    return (attention, d_qkv, totals[0], totals[1].reshape(head_count, span_count, span_count))


def solution(mesh):
    placed = (P("row", "col", None, None), P("row", "col", None), P(), P(), P(), P())
    return jax.shard_map(
        local,
        mesh=mesh,
        in_specs=placed,
        out_specs=(P("row", "col", None), P("row", "col", None, None), P(), P()),
        check_vma=False,
    )
```

profile of v0, /device:TPU:0, one launch (start us, length us, event | category | flops | bytes accessed | tf_op | source)
XLA Modules:
  0.0 298.4 jit_solution(15147776239652918049)
XLA Ops:
  0.6 1.5 pad_maximum_fusion
  2.2 5.5 %collective-permute-start = (bf16[8,8,4,3072]{3,1,2,0:T(8,128)(2,1)S(1)}, bf16[8,8,4,3072]{3,1,2,0:T(8,128)(2,1)}, u32[]{:S(2)}, u32[]{:S(2)}) collective-permute-start(bf16[8,8,4,3072]{3,1,2,0:T(8,128)(2,1)S(1)} %pad_maximum_fusion), channel_id=1, source_target_pairs={{0,30},{2,0},{4,2},{6,4},{8,6},{10,8},{12,10},{14,12},{16,14},{18,... | collective-permute-start | bytes 4718600 | tf_op jit(solution)/shard_map/ppermute | solution.py:14
  10.2 15.4 %collective-permute-done = bf16[8,8,4,3072]{3,1,2,0:T(8,128)(2,1)} collective-permute-done((bf16[8,8,4,3072]{3,1,2,0:T(8,128)(2,1)S(1)}, bf16[8,8,4,3072]{3,1,2,0:T(8,128)(2,1)}, u32[]{:S(2)}, u32[]{:S(2)}) %collective-permute-start) | collective-permute-done | bytes 1572896 | tf_op jit(solution)/shard_map/ppermute | solution.py:14
  25.6 2.9 fusion.5
  28.5 1.6 collective-permute-start.1
  33.5 0.9 iota_compare_fusion
  34.4 4.5 %fusion.20 = f32[24,64,64]{2,0,1:T(8,128)} fusion(pred[64,64,225]{2,0,1:T(32,128)(4,1)S(1)} %iota_compare_fusion, f32[24,225]{0,1:T(8,128)S(1)} %reshape.290), kind=kOutput, calls=%fused_computation.52 | convolution fusion | flops 265420800 | bytes 1336416 | tf_op jit(solution)/shard_map/hc,qkc->hqk/dot_general | solution.py:116
  38.9 2.3 copy.53
  42.4 0.7 broadcast_compare_fusion
  43.1 53.5 %collective-permute-done.1 = bf16[16,8,4,3072]{3,1,2,0:T(8,128)(2,1)} collective-permute-done((bf16[16,8,4,3072]{3,1,2,0:T(8,128)(2,1)S(1)}, bf16[16,8,4,3072]{3,1,2,0:T(8,128)(2,1)}, u32[]{:S(2)}, u32[]{:S(2)}) %collective-permute-start.1) | collective-permute-done | bytes 3145760 | tf_op jit(solution)/shard_map/ppermute | solution.py:14
  96.6 4.0 %fusion.7 = bf16[16,8,4,3072]{3,1,2,0:T(8,128)(2,1)S(1)} fusion(s32[]{:T(128)S(6)} %select_n.71, bf16[16,8,4,3072]{3,1,2,0:T(8,128)(2,1)S(1)} %fusion.5, bf16[16,8,4,3072]{3,1,2,0:T(8,128)(2,1)} %collective-permute-done.1), kind=kLoop, calls=%fused_computation.17 | loop fusion | flops 6291456 | bytes 9437188 | tf_op jit(solution)/shard_map/concatenate | solution.py:131
  100.6 0.9 copy.76
  101.5 0.9 convert_reduce_fusion
  102.4 2.4 fusion.38
  104.8 1.9 fusion.12
  107.0 4.2 %add_select_fusion = f32[2,24,64,64]{2,3,1,0:T(8,128)S(1)} fusion(f32[24,64,64]{1,2,0:T(8,128)} %copy.53, pred[2,64,64]{1,2,0:T(8,128)(4,1)} %broadcast_compare_fusion, f32[2,64,24,128]{3,2,1,0:T(8,128)} %bitcast.113, f32[128]{0:T(128)S(1)} %get-tuple-element.35, f32[2,64,24]{1,2,0:T(8,128)S(1)} %copy.47, f32[2,64,24]{1,2,0:T(8,128)S(1)} %copy.45, ...), kind=kOutput, calls=%fused_computation.44 | convolution fusion | flops 54067200 | bytes 4383744 | tf_op jit(solution)/shard_map/wqhd,wkhd->whqk/dot_general | solution.py:72
  111.2 1.6 fusion.40
  112.9 3.6 %fusion.19 = bf16[2,64,24,128]{3,1,2,0:T(8,128)(2,1)} fusion(bf16[2,64,24,128]{3,2,1,0:T(8,128)(2,1)} %bitcast.120, f32[2,24,64]{2,1,0:T(8,128)S(1)} %get-tuple-element.38, f32[2,24,64,64]{2,3,1,0:T(8,128)} %copy-done.2), kind=kOutput, calls=%fused_computation.51 | convolution fusion | flops 51317824 | bytes 2371584 | tf_op jit(solution)/shard_map/whqk,wqhd->wkhd/dot_general | solution.py:94
  116.5 3.6 %fusion.18 = bf16[2,64,24,128]{3,1,2,0:T(8,128)(2,1)} fusion(bf16[2,64,24,128]{3,2,1,0:T(8,128)(2,1)} %bitcast.122, f32[2,24,64]{2,1,0:T(8,128)S(1)} %get-tuple-element.38, f32[2,24,64,64]{2,3,1,0:T(8,128)} %copy-done.2), kind=kOutput, calls=%fused_computation.50 | convolution fusion | flops 51317824 | bytes 2371584 | tf_op jit(solution)/shard_map/whqk,wkhd->wqhd/dot_general | solution.py:81
  120.1 2.5 copy.56
  122.6 2.2 stack.22
  124.8 2.5 copy.69
  127.3 2.2 stack.25
  129.5 2.6 multiply_reduce_fusion.2
  132.1 1.4 fusion.29
  133.5 0.7 copy-done.4
  134.2 4.8 %multiply_reduce_fusion = (f32[128]{0:T(128)}, f32[2,64,24]{1,2,0:T(8,128)S(1)}, f32[2,64,24]{1,2,0:T(8,128)S(1)}, f32[2,24,128,64]{2,3,1,0:T(8,128)}) fusion(f32[2,64,24,128]{3,2,1,0:T(8,128)S(1)} %bitcast.111, f32[2,64,24]{1,2,0:T(8,128)S(1)} %copy.50, f32[2,64,24]{1,2,0:T(8,128)S(1)} %copy.48, f32[128]{0:T(128)S(1)} %copy-done.20, ...), kind=kOutput, calls=%fused_computation.36 | convolution fusion | flops 55437184 | bytes 5187072 | tf_op jit(solution)/shard_map/whqk,wqhd->wkhd/dot_general | solution.py:91
  139.0 5.3 %multiply_reduce_fusion.1 = (f32[128]{0:T(128)}, f32[2,64,24]{1,2,0:T(8,128)S(1)}, f32[2,64,24]{1,2,0:T(8,128)S(1)}, f32[2,24,128,64]{2,3,1,0:T(8,128)}) fusion(f32[2,64,24,128]{3,2,1,0:T(8,128)S(1)} %bitcast.115, f32[2,64,24]{1,2,0:T(8,128)S(1)} %copy.47, f32[2,64,24]{1,2,0:T(8,128)S(1)} %copy.45, f32[128]{0:T(128)S(1)} %copy-done.19, ...), kind=kOutput, calls=%fused_computation.37 | convolution fusion | flops 55437184 | bytes 5187072 | tf_op jit(solution)/shard_map/whqk,wkhd->wqhd/dot_general | solution.py:87
  144.9 0.6 broadcast_multiply_fusion.3
  146.2 0.8 copy.63
  147.1 1.4 copy.66
  148.5 1.4 copy.67
  149.9 1.6 multiply_bitcast_fusion
  151.5 0.9 copy.64
  153.2 0.9 copy.60
  154.1 5.1 %multiply_convert_fusion = (bf16[16,8,1,24,128]{4,3,1,2,0:T(8,128)(2,1)}, bf16[16,8,1,24,128]{4,3,1,2,0:T(8,128)(2,1)}) fusion(f32[16,8,1,24,128]{4,3,1,2,0:T(8,128)S(1)} %bitcast.108, f32[16,8,24]{2,1,0:T(8,128)S(1)} %bitcast.129, f32[16,8,24]{2,1,0:T(8,128)S(1)} %get-tuple-element.46, f32[16,8,24]{2,1,0:T(8,128)S(1)} %bitcast.128, ...), kind=kLoop, calls=%fused_computation.38 | loop fusion | flops 7077888 | bytes 6390784 | tf_op jit(solution)/shard_map/convert.8
  159.2 1.5 stack.24
  161.3 1.0 copy-done.5
  162.5 1.5 copy-done
  165.4 21.3 %collective-permute-done.2 = bf16[8,8,4,3072]{3,1,0,2:T(8,128)(2,1)} collective-permute-done((bf16[8,8,4,3072]{3,1,0,2:T(8,128)(2,1)S(1)}, bf16[8,8,4,3072]{3,1,0,2:T(8,128)(2,1)}, u32[]{:S(2)}, u32[]{:S(2)}) %collective-permute-start.2) | collective-permute-done | bytes 1572896 | tf_op jit(solution)/shard_map/ppermute | solution.py:14
  186.7 2.6 fusion.3
  189.3 1.6 collective-permute-start.3
  192.1 2.8 convolution_bitcast_fusion
  195.0 95.8 %all-reduce = (f32[2,128]{1,0:T(2,128)}, f32[24,15,15]{2,1,0:T(8,128)S(1)}) all-reduce(f32[2,128]{1,0:T(2,128)S(1)} %pad_maximum_fusion.1, f32[24,15,15]{2,1,0:T(8,128)S(1)} %reshape.285), channel_id=1, replica_groups=mesh['row'=16,'col'=2] {'row','col'}, use_global_device_ids=true, to_apply=%region_13.14 | all-reduce | flops 5656 | bytes 45248 | tf_op jit(solution)/shard_map/psum | solution.py:170
  290.9 0.8 copy.72
  291.7 4.0 %fusion.6 = bf16[16,8,4,3072]{3,1,0,2:T(8,128)(2,1)S(1)} fusion(s32[]{:T(128)S(6)} %select_n.80, bf16[16,8,4,3072]{3,1,0,2:T(8,128)(2,1)} %collective-permute-done.3, bf16[16,8,4,3072]{3,1,0,2:T(8,128)(2,1)S(1)} %fusion.3), kind=kLoop, calls=%fused_computation.16 | loop fusion | flops 6291456 | bytes 9437188 | tf_op jit(solution)/shard_map/concatenate | solution.py:165
  295.8 0.9 slice_bitcast_fusion
  296.8 1.6 copy.71
  (72 shorter events, 5.5 us)
Async XLA Ops:
  0.6 7.1 %copy-start.16 = (s32[2]{0:T(128)S(1)}, s32[2]{0:T(128)}, u32[]{:S(2)}) copy-start(s32[2]{0:T(128)} %param.10) | copy-start | bytes 28
  2.2 23.4 %collective-permute-start = (bf16[8,8,4,3072]{3,1,2,0:T(8,128)(2,1)S(1)}, bf16[8,8,4,3072]{3,1,2,0:T(8,128)(2,1)}, u32[]{:S(2)}, u32[]{:S(2)}) collective-permute-start(bf16[8,8,4,3072]{3,1,2,0:T(8,128)(2,1)S(1)} %pad_maximum_fusion), channel_id=1, source_target_pairs={{0,30},{2,0},{4,2},{6,4},{8,6},{10,8},{12,10},{14,12},{16,14},{18,... | collective-permute-start | bytes 4718600 | tf_op jit(solution)/shard_map/ppermute | solution.py:14
  10.2 22.3 %copy-start.14 = (s32[256,16]{0,1:T(8,128)S(1)}, s32[256,16]{0,1:T(8,128)}, u32[]{:S(2)}) copy-start(s32[256,16]{0,1:T(8,128)} %param.11) | copy-start | bytes 49156
  10.2 22.5 %copy-start.13 = (f32[24,15,15]{0,2,1:T(8,128)S(1)}, f32[24,15,15]{0,2,1:T(8,128)}, u32[]{:S(2)}) copy-start(f32[24,15,15]{0,2,1:T(8,128)} %param.9) | copy-start | bytes 64804
  28.5 68.1 %collective-permute-start.1 = (bf16[16,8,4,3072]{3,1,2,0:T(8,128)(2,1)S(1)}, bf16[16,8,4,3072]{3,1,2,0:T(8,128)(2,1)}, u32[]{:S(2)}, u32[]{:S(2)}) collective-permute-start(bf16[16,8,4,3072]{3,1,2,0:T(8,128)(2,1)S(1)} %fusion.5), channel_id=1, source_target_pairs={{0,1},{1,0},{2,3},{3,2},{4,5},{5,4},{6,7},{7,6},{8,9},{9,8},{10,11... | collective-permute-start | bytes 9437192 | tf_op jit(solution)/shard_map/ppermute | solution.py:14
  32.9 0.6 copy-start.11
  38.9 2.9 copy-start.15
  111.2 1.7 copy-start.2
  129.5 2.6 copy-start.1
  132.1 1.4 copy-start.3
  132.1 2.2 copy-start.4
  132.1 2.1 copy-start.20
  134.2 4.8 %copy-start.19 = (f32[128]{0:T(128)S(1)}, f32[128]{0:T(128)}, u32[]{:S(2)}) copy-start(f32[128]{0:T(128)} %get-tuple-element.33) | copy-start | bytes 1540
  151.5 1.4 copy-start.8
  153.2 0.9 copy-start.9
  153.2 0.9 copy-start.10
  159.2 1.6 copy-start.7
  159.2 1.9 copy-start.6
  161.2 1.1 copy-start.5
  162.4 1.7 copy-start
  164.1 22.6 %collective-permute-start.2 = (bf16[8,8,4,3072]{3,1,0,2:T(8,128)(2,1)S(1)}, bf16[8,8,4,3072]{3,1,0,2:T(8,128)(2,1)}, u32[]{:S(2)}, u32[]{:S(2)}) collective-permute-start(bf16[8,8,4,3072]{3,1,0,2:T(8,128)(2,1)S(1)} %slice.56), channel_id=1, source_target_pairs={{0,2},{2,4},{4,6},{6,8},{8,10},{10,12},{12,14},{14,16},{16,18},{18... | collective-permute-start | bytes 4718600 | tf_op jit(solution)/shard_map/ppermute | solution.py:14
  165.4 26.7 %copy-start.12 = (s32[64,64]{0,1:T(8,128)S(1)}, s32[64,64]{0,1:T(8,128)}, u32[]{:S(2)}) copy-start(s32[64,64]{0,1:T(8,128)} %copy-done.11) | copy-start | bytes 49156
  189.3 5.7 %copy-start.17 = (f32[128]{0:T(128)S(1)}, f32[128]{0:T(128)}, u32[]{:S(2)}) copy-start(f32[128]{0:T(128)} %get-tuple-element.14) | copy-start | bytes 1540
  189.3 5.7 %copy-start.18 = (f32[128]{0:T(128)S(1)}, f32[128]{0:T(128)}, u32[]{:S(2)}) copy-start(f32[128]{0:T(128)} %get-tuple-element.12) | copy-start | bytes 1540
  189.3 102.4 %collective-permute-start.3 = (bf16[16,8,4,3072]{3,1,0,2:T(8,128)(2,1)S(1)}, bf16[16,8,4,3072]{3,1,0,2:T(8,128)(2,1)}, u32[]{:S(2)}, u32[]{:S(2)}) collective-permute-start(bf16[16,8,4,3072]{3,1,0,2:T(8,128)(2,1)S(1)} %fusion.3), channel_id=1, source_target_pairs={{0,1},{1,0},{2,3},{3,2},{4,5},{5,4},{6,7},{7,6},{8,9},{9,8},{10,11... | collective-permute-start | bytes 9437192 | tf_op jit(solution)/shard_map/ppermute | solution.py:14
where the time goes:
time: 299 us; the launch traced here: 298 us
  blocking collectives  95.8 us (32%)
  waiting for transfers between devices  90.2 us (30%)
  other arithmetic  34.4 us (12%)
  matrix products  31.4 us (11%)
  local copies, waits for them, and re-layouts  29.4 us (10%)
  starting transfers between devices  8.67 us (3%)
  between operations  8.46 us (3%)
    psum x1, blocking collectives, local(): lax.psum((jnp.stack([dgain_q, dgain_k]), table_local), ('row', 'col'))  95.8 us
    ppermute x4, waiting for transfers between devices, shifted(): return lax.ppermute(value, axis, pairs)  90.2 us
    ppermute x4, starting transfers between devices, shifted(): return lax.ppermute(value, axis, pairs)  8.67 us
    unnamed x48, local copies, waits for them, and re-layouts  7.83 us
    another operation x5, local copies, waits for them, and re-layouts, local(): jnp.stack([output, d_query, d_key, d_value], axis=2)  6.26 us
  transfers between devices with their start and end apart: 4, of which 3 were waited for; matrix products, arithmetic and copies ran while one was open for 5% of the time, Pallas kernels for 0%

commit v1 on v0

--- a/solution.py
+++ b/solution.py
@@ -167,7 +167,9 @@
     attention = results[:, :, 0]
     d_qkv = results[:, :, 1:]
     table_local = jnp.einsum("hqk,qkc->hc", d_bias, one_hot, precision=lax.Precision.HIGHEST)
-    totals = lax.psum((jnp.stack([dgain_q, dgain_k]), table_local), ("row", "col"))
+    totals = (jnp.stack([dgain_q, dgain_k]), table_local)
+    for to_i in ("row", "col"):
+        totals = lax.psum(totals, axis_name=to_i)
     return (attention, d_qkv, totals[0], totals[1].reshape(head_count, span_count, span_count))
 
 

time: 299 us -> 271 us (0.906)
  blocking collectives: 95.8 us -> 67.6 us
    psum x1 -> x2, blocking collectives: 95.8 us -> 67.6 us  [local(): totals = lax.psum(totals, axis_name=to_i)]
where the time goes in v1:
time: 271 us; the launch traced here: 270 us
  waiting for transfers between devices  90.2 us (33%)
  blocking collectives  67.6 us (25%)
  other arithmetic  34.4 us (13%)
  matrix products  31.4 us (12%)
  local copies, waits for them, and re-layouts  29.4 us (11%)
  starting transfers between devices  8.67 us (3%)
  between operations  8.45 us (3%)
    ppermute x4, waiting for transfers between devices, shifted(): return lax.ppermute(value, axis, pairs)  90.2 us
    psum x2, blocking collectives, local(): totals = lax.psum(totals, axis_name=to_i)  67.6 us
    ppermute x4, starting transfers between devices, shifted(): return lax.ppermute(value, axis, pairs)  8.67 us
    unnamed x48, local copies, waits for them, and re-layouts  7.83 us
    another operation x5, local copies, waits for them, and re-layouts, local(): jnp.stack([output, d_query, d_key, d_value], axis=2)  6.26 us
  transfers between devices with their start and end apart: 4, of which 3 were waited for; matrix products, arithmetic and copies ran while one was open for 5% of the time, Pallas kernels for 0%

profile of v1, /device:TPU:0, one launch (start us, length us, event | category | flops | bytes accessed | tf_op | source)
XLA Modules:
  0.0 270.1 jit_solution(16778575518963920189)
XLA Ops:
  0.6 1.5 pad_maximum_fusion
  2.2 5.5 %collective-permute-start = (bf16[8,8,4,3072]{3,1,2,0:T(8,128)(2,1)S(1)}, bf16[8,8,4,3072]{3,1,2,0:T(8,128)(2,1)}, u32[]{:S(2)}, u32[]{:S(2)}) collective-permute-start(bf16[8,8,4,3072]{3,1,2,0:T(8,128)(2,1)S(1)} %pad_maximum_fusion), channel_id=1, source_target_pairs={{0,30},{2,0},{4,2},{6,4},{8,6},{10,8},{12,10},{14,12},{16,14},{18,... | collective-permute-start | bytes 4718600 | tf_op jit(solution)/shard_map/ppermute | solution.py:14
  10.2 15.4 %collective-permute-done = bf16[8,8,4,3072]{3,1,2,0:T(8,128)(2,1)} collective-permute-done((bf16[8,8,4,3072]{3,1,2,0:T(8,128)(2,1)S(1)}, bf16[8,8,4,3072]{3,1,2,0:T(8,128)(2,1)}, u32[]{:S(2)}, u32[]{:S(2)}) %collective-permute-start) | collective-permute-done | bytes 1572896 | tf_op jit(solution)/shard_map/ppermute | solution.py:14
  25.6 2.9 %fusion.5 = bf16[16,8,4,3072]{3,1,2,0:T(8,128)(2,1)S(1)} fusion(s32[]{:T(128)S(6)} %select_n.70, bf16[16,8,3,3072]{3,1,2,0:T(8,128)(2,1)} %param.6, bf16[16,8,1,3072]{3,1,2,0:T(8,128)(2,1)} %bitcast.117, bf16[8,8,4,3072]{3,1,2,0:T(8,128)(2,1)} %collective-permute-done), kind=kLoop, calls=%fused_computation.15 | loop fusion | flops 3145728 | bytes 7864324 | tf_op jit(solution)/shard_map/concatenate | solution.py:127
  28.5 1.6 collective-permute-start.1
  33.5 0.9 iota_compare_fusion
  34.4 4.5 %fusion.20 = f32[24,64,64]{2,0,1:T(8,128)} fusion(pred[64,64,225]{2,0,1:T(32,128)(4,1)S(1)} %iota_compare_fusion, f32[24,225]{0,1:T(8,128)S(1)} %reshape.290), kind=kOutput, calls=%fused_computation.52 | convolution fusion | flops 265420800 | bytes 1336416 | tf_op jit(solution)/shard_map/hc,qkc->hqk/dot_general | solution.py:116
  38.9 2.3 copy.53
  42.4 0.7 broadcast_compare_fusion
  43.1 53.5 %collective-permute-done.1 = bf16[16,8,4,3072]{3,1,2,0:T(8,128)(2,1)} collective-permute-done((bf16[16,8,4,3072]{3,1,2,0:T(8,128)(2,1)S(1)}, bf16[16,8,4,3072]{3,1,2,0:T(8,128)(2,1)}, u32[]{:S(2)}, u32[]{:S(2)}) %collective-permute-start.1) | collective-permute-done | bytes 3145760 | tf_op jit(solution)/shard_map/ppermute | solution.py:14
  96.6 4.0 %fusion.7 = bf16[16,8,4,3072]{3,1,2,0:T(8,128)(2,1)S(1)} fusion(s32[]{:T(128)S(6)} %select_n.71, bf16[16,8,4,3072]{3,1,2,0:T(8,128)(2,1)S(1)} %fusion.5, bf16[16,8,4,3072]{3,1,2,0:T(8,128)(2,1)} %collective-permute-done.1), kind=kLoop, calls=%fused_computation.17 | loop fusion | flops 6291456 | bytes 9437188 | tf_op jit(solution)/shard_map/concatenate | solution.py:131
  100.6 0.9 copy.76
  101.5 0.9 convert_reduce_fusion
  102.4 2.4 fusion.38
  104.8 1.9 fusion.12
  107.0 4.2 %add_select_fusion = f32[2,24,64,64]{2,3,1,0:T(8,128)S(1)} fusion(f32[24,64,64]{1,2,0:T(8,128)} %copy.53, pred[2,64,64]{1,2,0:T(8,128)(4,1)} %broadcast_compare_fusion, f32[2,64,24,128]{3,2,1,0:T(8,128)} %bitcast.113, f32[128]{0:T(128)S(1)} %get-tuple-element.37, f32[2,64,24]{1,2,0:T(8,128)S(1)} %copy.47, f32[2,64,24]{1,2,0:T(8,128)S(1)} %copy.45, ...), kind=kOutput, calls=%fused_computation.44 | convolution fusion | flops 54067200 | bytes 4383744 | tf_op jit(solution)/shard_map/wqhd,wkhd->whqk/dot_general | solution.py:72
  111.2 1.6 fusion.40
  112.9 3.6 %fusion.19 = bf16[2,64,24,128]{3,1,2,0:T(8,128)(2,1)} fusion(bf16[2,64,24,128]{3,2,1,0:T(8,128)(2,1)} %bitcast.120, f32[2,24,64]{2,1,0:T(8,128)S(1)} %get-tuple-element.40, f32[2,24,64,64]{2,3,1,0:T(8,128)} %copy-done.2), kind=kOutput, calls=%fused_computation.51 | convolution fusion | flops 51317824 | bytes 2371584 | tf_op jit(solution)/shard_map/whqk,wqhd->wkhd/dot_general | solution.py:94
  116.5 3.6 %fusion.18 = bf16[2,64,24,128]{3,1,2,0:T(8,128)(2,1)} fusion(bf16[2,64,24,128]{3,2,1,0:T(8,128)(2,1)} %bitcast.122, f32[2,24,64]{2,1,0:T(8,128)S(1)} %get-tuple-element.40, f32[2,24,64,64]{2,3,1,0:T(8,128)} %copy-done.2), kind=kOutput, calls=%fused_computation.50 | convolution fusion | flops 51317824 | bytes 2371584 | tf_op jit(solution)/shard_map/whqk,wkhd->wqhd/dot_general | solution.py:81
  120.1 2.5 copy.56
  122.6 2.2 stack.22
  124.8 2.5 copy.69
  127.3 2.2 stack.25
  129.5 2.6 multiply_reduce_fusion.2
  132.1 1.4 fusion.29
  133.5 0.7 copy-done.4
  134.2 4.8 %multiply_reduce_fusion = (f32[128]{0:T(128)}, f32[2,64,24]{1,2,0:T(8,128)S(1)}, f32[2,64,24]{1,2,0:T(8,128)S(1)}, f32[2,24,128,64]{2,3,1,0:T(8,128)}) fusion(f32[2,64,24,128]{3,2,1,0:T(8,128)S(1)} %bitcast.111, f32[2,64,24]{1,2,0:T(8,128)S(1)} %copy.50, f32[2,64,24]{1,2,0:T(8,128)S(1)} %copy.48, f32[128]{0:T(128)S(1)} %copy-done.20, ...), kind=kOutput, calls=%fused_computation.36 | convolution fusion | flops 55437184 | bytes 5187072 | tf_op jit(solution)/shard_map/whqk,wqhd->wkhd/dot_general | solution.py:91
  139.0 5.3 %multiply_reduce_fusion.1 = (f32[128]{0:T(128)}, f32[2,64,24]{1,2,0:T(8,128)S(1)}, f32[2,64,24]{1,2,0:T(8,128)S(1)}, f32[2,24,128,64]{2,3,1,0:T(8,128)}) fusion(f32[2,64,24,128]{3,2,1,0:T(8,128)S(1)} %bitcast.115, f32[2,64,24]{1,2,0:T(8,128)S(1)} %copy.47, f32[2,64,24]{1,2,0:T(8,128)S(1)} %copy.45, f32[128]{0:T(128)S(1)} %copy-done.19, ...), kind=kOutput, calls=%fused_computation.37 | convolution fusion | flops 55437184 | bytes 5187072 | tf_op jit(solution)/shard_map/whqk,wkhd->wqhd/dot_general | solution.py:87
  146.2 0.8 copy.63
  147.1 1.4 copy.66
  148.5 1.4 copy.67
  149.9 1.6 multiply_bitcast_fusion
  151.5 0.9 copy.64
  153.2 0.9 copy.60
  154.1 5.1 %multiply_convert_fusion = (bf16[16,8,1,24,128]{4,3,1,2,0:T(8,128)(2,1)}, bf16[16,8,1,24,128]{4,3,1,2,0:T(8,128)(2,1)}) fusion(f32[16,8,1,24,128]{4,3,1,2,0:T(8,128)S(1)} %bitcast.108, f32[16,8,24]{2,1,0:T(8,128)S(1)} %bitcast.129, f32[16,8,24]{2,1,0:T(8,128)S(1)} %get-tuple-element.48, f32[16,8,24]{2,1,0:T(8,128)S(1)} %bitcast.128, ...), kind=kLoop, calls=%fused_computation.38 | loop fusion | flops 7077888 | bytes 6390784 | tf_op jit(solution)/shard_map/convert.8
  159.2 1.5 stack.24
  161.3 1.0 copy-done.5
  162.5 1.5 copy-done
  165.4 21.3 %collective-permute-done.2 = bf16[8,8,4,3072]{3,1,0,2:T(8,128)(2,1)} collective-permute-done((bf16[8,8,4,3072]{3,1,0,2:T(8,128)(2,1)S(1)}, bf16[8,8,4,3072]{3,1,0,2:T(8,128)(2,1)}, u32[]{:S(2)}, u32[]{:S(2)}) %collective-permute-start.2) | collective-permute-done | bytes 1572896 | tf_op jit(solution)/shard_map/ppermute | solution.py:14
  186.7 2.6 fusion.3
  189.3 1.6 collective-permute-start.3
  192.1 2.8 %convolution_bitcast_fusion = f32[24,225]{1,0:T(8,128)S(1)} fusion(f32[24,64,64]{1,2,0:T(8,128)} %get-tuple-element.26, s32[64,64]{0,1:T(8,128)S(1)} %copy-done.12), kind=kOutput, calls=%fused_computation.55 | convolution fusion | flops 266342400 | bytes 431200 | tf_op jit(solution)/shard_map/hqk,qkc->hc/dot_general | solution.py:169
  194.9 57.6 %all-reduce = (f32[2,128]{1,0:T(2,128)S(1)}, f32[24,225]{1,0:T(8,128)S(1)}) all-reduce(f32[2,128]{1,0:T(2,128)S(1)} %pad_maximum_fusion.1, f32[24,225]{1,0:T(8,128)S(1)} %convolution_bitcast_fusion), channel_id=1, replica_groups=mesh['row'=16,'col'=2] {'row'}, use_global_device_ids=true, to_apply=%region_13.14 | all-reduce | flops 5656 | bytes 45248 | tf_op jit(solution)/shard_map/psum | solution.py:172
  252.7 10.0 %all-reduce.1 = (f32[2,128]{1,0:T(2,128)}, f32[24,15,15]{2,1,0:T(8,128)S(1)}) all-reduce(f32[2,128]{1,0:T(2,128)S(1)} %get-tuple-element.22, f32[24,15,15]{2,1,0:T(8,128)S(1)} %reshape.285), channel_id=1, replica_groups=mesh['row'=16,'col'=2] {'col'}, use_global_device_ids=true, to_apply=%region_14.15 | all-reduce | flops 5656 | bytes 45248 | tf_op jit(solution)/shard_map/psum | solution.py:172
  262.6 0.8 copy.72
  263.4 4.0 %fusion.6 = bf16[16,8,4,3072]{3,1,0,2:T(8,128)(2,1)S(1)} fusion(s32[]{:T(128)S(6)} %select_n.80, bf16[16,8,4,3072]{3,1,0,2:T(8,128)(2,1)} %collective-permute-done.3, bf16[16,8,4,3072]{3,1,0,2:T(8,128)(2,1)S(1)} %fusion.3), kind=kLoop, calls=%fused_computation.16 | loop fusion | flops 6291456 | bytes 9437188 | tf_op jit(solution)/shard_map/concatenate | solution.py:165
  267.5 0.9 slice_bitcast_fusion
  268.6 1.6 copy.71
  (73 shorter events, 6.1 us)
Async XLA Ops:
  0.6 7.1 %copy-start.16 = (s32[2]{0:T(128)S(1)}, s32[2]{0:T(128)}, u32[]{:S(2)}) copy-start(s32[2]{0:T(128)} %param.10) | copy-start | bytes 28
  2.2 23.4 %collective-permute-start = (bf16[8,8,4,3072]{3,1,2,0:T(8,128)(2,1)S(1)}, bf16[8,8,4,3072]{3,1,2,0:T(8,128)(2,1)}, u32[]{:S(2)}, u32[]{:S(2)}) collective-permute-start(bf16[8,8,4,3072]{3,1,2,0:T(8,128)(2,1)S(1)} %pad_maximum_fusion), channel_id=1, source_target_pairs={{0,30},{2,0},{4,2},{6,4},{8,6},{10,8},{12,10},{14,12},{16,14},{18,... | collective-permute-start | bytes 4718600 | tf_op jit(solution)/shard_map/ppermute | solution.py:14
  10.2 22.3 %copy-start.14 = (s32[256,16]{0,1:T(8,128)S(1)}, s32[256,16]{0,1:T(8,128)}, u32[]{:S(2)}) copy-start(s32[256,16]{0,1:T(8,128)} %param.11) | copy-start | bytes 49156
  10.2 22.5 %copy-start.13 = (f32[24,15,15]{0,2,1:T(8,128)S(1)}, f32[24,15,15]{0,2,1:T(8,128)}, u32[]{:S(2)}) copy-start(f32[24,15,15]{0,2,1:T(8,128)} %param.9) | copy-start | bytes 64804
  28.5 68.1 %collective-permute-start.1 = (bf16[16,8,4,3072]{3,1,2,0:T(8,128)(2,1)S(1)}, bf16[16,8,4,3072]{3,1,2,0:T(8,128)(2,1)}, u32[]{:S(2)}, u32[]{:S(2)}) collective-permute-start(bf16[16,8,4,3072]{3,1,2,0:T(8,128)(2,1)S(1)} %fusion.5), channel_id=1, source_target_pairs={{0,1},{1,0},{2,3},{3,2},{4,5},{5,4},{6,7},{7,6},{8,9},{9,8},{10,11... | collective-permute-start | bytes 9437192 | tf_op jit(solution)/shard_map/ppermute | solution.py:14
  32.9 0.6 copy-start.11
  38.9 2.9 %copy-start.15 = (f32[2,128]{1,0:T(2,128)S(1)}, f32[2,128]{1,0:T(2,128)}, u32[]{:S(2)}) copy-start(f32[2,128]{1,0:T(2,128)} %param.8) | copy-start | bytes 3076
  111.2 1.7 copy-start.2
  129.5 2.6 copy-start.1
  132.1 1.4 copy-start.3
  132.1 2.2 copy-start.4
  132.1 2.1 copy-start.20
  134.2 4.8 %copy-start.19 = (f32[128]{0:T(128)S(1)}, f32[128]{0:T(128)}, u32[]{:S(2)}) copy-start(f32[128]{0:T(128)} %get-tuple-element.35) | copy-start | bytes 1540
  151.5 1.4 copy-start.8
  153.2 0.9 copy-start.9
  153.2 0.9 copy-start.10
  159.2 1.6 copy-start.7
  159.2 1.9 copy-start.6
  161.2 1.1 copy-start.5
  162.4 1.7 copy-start
  164.1 22.6 %collective-permute-start.2 = (bf16[8,8,4,3072]{3,1,0,2:T(8,128)(2,1)S(1)}, bf16[8,8,4,3072]{3,1,0,2:T(8,128)(2,1)}, u32[]{:S(2)}, u32[]{:S(2)}) collective-permute-start(bf16[8,8,4,3072]{3,1,0,2:T(8,128)(2,1)S(1)} %slice.56), channel_id=1, source_target_pairs={{0,2},{2,4},{4,6},{6,8},{8,10},{10,12},{12,14},{14,16},{16,18},{18... | collective-permute-start | bytes 4718600 | tf_op jit(solution)/shard_map/ppermute | solution.py:14
  165.4 26.7 %copy-start.17 = (f32[128]{0:T(128)S(1)}, f32[128]{0:T(128)}, u32[]{:S(2)}) copy-start(f32[128]{0:T(128)} %get-tuple-element.14) | copy-start | bytes 1540
  165.4 26.7 %copy-start.18 = (f32[128]{0:T(128)S(1)}, f32[128]{0:T(128)}, u32[]{:S(2)}) copy-start(f32[128]{0:T(128)} %get-tuple-element.12) | copy-start | bytes 1540
  165.4 26.7 %copy-start.12 = (s32[64,64]{0,1:T(8,128)S(1)}, s32[64,64]{0,1:T(8,128)}, u32[]{:S(2)}) copy-start(s32[64,64]{0,1:T(8,128)} %copy-done.11) | copy-start | bytes 49156
  189.3 74.1 %collective-permute-start.3 = (bf16[16,8,4,3072]{3,1,0,2:T(8,128)(2,1)S(1)}, bf16[16,8,4,3072]{3,1,0,2:T(8,128)(2,1)}, u32[]{:S(2)}, u32[]{:S(2)}) collective-permute-start(bf16[16,8,4,3072]{3,1,0,2:T(8,128)(2,1)S(1)} %fusion.3), channel_id=1, source_target_pairs={{0,1},{1,0},{2,3},{3,2},{4,5},{5,4},{6,7},{7,6},{8,9},{9,8},{10,11... | collective-permute-start | bytes 9437192 | tf_op jit(solution)/shard_map/ppermute | solution.py:14
